TPU v7x, 32 devices: a whole 2x2x4 slice. The times are simulated.
32 devices in a mesh: win: 2 (over y), row: 16 (over z, x, core).
Axes of the slice: x: 2, y: 2, z: 4, core: 2. Of those that a mesh axis runs over, the one named last changes fastest.
Arguments:
- raw: bfloat16 [4096, 16384], P(None, ('win', 'row')), parts along dimension 1, may hold values from -30 to 30, as said below
- fir_taps: float32 [16], replicated, may hold values from -1.5 to 1.5
- band_width: int32 [16], P('row'), may hold values from 1 to 8, as said below
- dead_count: int32 [16], P('row'), may hold values from 0 to 64, as said below
Outputs:
- correlations: bfloat16 [8192, 8, 8, 256], P(('win', 'row')), parts along dimension 0
There are 2 independent parts, one for each index of `win`. A program takes and returns all parts, laid end to end along the dimension named above; an argument that names none is the same for every part. Nothing has to cross between parts.
Inputs may be any that keep to these rules, and one draw needn't show every extreme that they name: `raw`: samples of the record. Row tile t pairs with column tiles t to t + band_width[t] - 1; band_width[t] <= 16 - t, and tile 0 pairs with 8 tiles. `dead_count`: some tile has 64 dead channels.
All inputs are finite; a program needn't handle non-finite values.
Results may differ from a plain program's by a relative error of at most 0.0069.
Values may be sent and summed in bfloat16 or wider, within the bound.
No kernel may reach another device: no remote copies, remote signals or barrier semaphores. Data moves between devices by JAX's collectives and lax.ppermute only.
A program may use at most 128 MiB of HBM per device.

v0:
```python
import math
import jax
import jax.numpy as jnp
from jax import lax
from jax.sharding import PartitionSpec as P

NT = 2048
NF = 512
DEC = 4
TAPS = 16
SMOOTH = 64
LAGS = 8
NB = 8


def from_behind(value, axis, steps):
    count = lax.axis_size(axis)
    initial, last = (max(0, -steps), min(count, count - steps))
    return lax.ppermute(value, axis, [(source, source + steps) for source in range(initial, last)])


def fir_decimate(padded, fir_taps, count):
    left_reach = (TAPS - DEC) // 2
    rows = padded.shape[0]
    width = padded.shape[1]
    phased = jnp.transpose(padded.reshape(rows, width // DEC, DEC), (2, 0, 1))
    filtered = jnp.zeros((rows, count), jnp.float32)
    for tap_index in range(TAPS):
        first_at = 2 * DEC - left_reach + tap_index
        phase_index = first_at % DEC
        block_start = first_at // DEC
        sampled = phased[phase_index, :, block_start : block_start + count]
        filtered = filtered + fir_taps[tap_index] * sampled
    return filtered


def spectral_table():
    sample_ids = jnp.arange(NT, dtype=jnp.int32)[:, None]
    bin_ids = jnp.arange(NF, dtype=jnp.int32)[None, :] + 1
    phases = (sample_ids * bin_ids % NT).astype(jnp.float32) * (2.0 * math.pi / NT)
    return jnp.concatenate([jnp.cos(phases), -jnp.sin(phases)], axis=1).astype(jnp.bfloat16)


def whiten(decimated):
    spectrum = jnp.dot(decimated, spectral_table(), preferred_element_type=jnp.float32)
    real_part = spectrum[:, :NF]
    imag_part = spectrum[:, NF:]
    power_bins = real_part * real_part + imag_part * imag_part
    bin_ids = jnp.arange(NF, dtype=jnp.int32)
    window = (jnp.abs(bin_ids[:, None] - bin_ids[None, :]) <= SMOOTH).astype(jnp.float32)
    counts = jnp.sum(window, axis=0)
    smoothed = (
        jnp.dot(
            power_bins, window, precision=lax.Precision.HIGHEST, preferred_element_type=jnp.float32
        )
        / counts
    )
    factor = lax.rsqrt(smoothed + 1e-05)
    return (real_part * factor, imag_part * factor)


def lag_rows(white_real, white_imag):
    lag_ids = jnp.arange(LAGS, dtype=jnp.int32) - LAGS // 2
    bin_ids = jnp.arange(NF, dtype=jnp.int32) + 1
    phases = ((lag_ids % NT)[:, None] * bin_ids[None, :] % NT).astype(jnp.float32) * (
        2.0 * math.pi / NT
    )
    cosine_table = jnp.cos(phases)[None]
    sine_table = jnp.sin(phases)[None]
    rotated_real = white_real[:, None, :] * cosine_table - white_imag[:, None, :] * sine_table
    rotated_imag = white_real[:, None, :] * sine_table + white_imag[:, None, :] * cosine_table
    stacked = jnp.concatenate([rotated_real, rotated_imag], axis=2).astype(jnp.bfloat16)
    return stacked.reshape(-1, 2 * NF)


def shards(raw, fir_taps, band_width, dead_count):
    band_span = band_width[0]
    dead_here = dead_count[0]
    channel_block = lax.all_to_all(raw, "row", split_axis=0, concat_axis=1, tiled=True)
    padded = jnp.pad(channel_block.astype(jnp.float32), ((0, 0), (2 * DEC, 2 * DEC)))
    filtered = fir_decimate(padded, fir_taps, NT)
    tile_rows = filtered.shape[0]
    keep_mask = (jnp.arange(tile_rows, dtype=jnp.int32) >= dead_here).astype(jnp.float32)[:, None]
    decimated = (filtered * keep_mask).astype(jnp.bfloat16)
    white_real, white_imag = whiten(decimated)
    white = jnp.concatenate([white_real, white_imag], axis=1).astype(jnp.bfloat16)
    lagged = lag_rows(white_real, white_imag)
    column_list = [white]
    for offset in range(1, NB):
        column_list.append(from_behind(white, "row", -offset))
    window_tiles = jnp.stack(column_list, axis=0)
    scales = (jnp.arange(NB, dtype=jnp.int32) < band_span).astype(jnp.float32) / math.sqrt(NF)
    column_block = window_tiles.reshape(NB * tile_rows, 2 * NF)
    product = lax.dot_general(
        lagged, column_block, (((1,), (1,)), ((), ())), preferred_element_type=jnp.float32
    )
    shaped = product.reshape(tile_rows, LAGS, NB, tile_rows)
    return (shaped * scales[None, None, :, None]).astype(jnp.bfloat16)


def solution(mesh):
    return jax.shard_map(
        shards,
        mesh=mesh,
        in_specs=(P(None, ("win", "row")), P(), P("row"), P("row")),
        out_specs=P(("win", "row"), None, None, None),
        check_vma=False,
    )
```

profile of v0, /device:TPU:1, one launch (start us, length us, event | category | flops | bytes accessed | tf_op | source)
XLA Modules:
  0.0 294.4 jit_solution(10741575521673612)
XLA Ops:
  0.0 0.0 copy-start
  0.0 7.5 %all-to-all-start = ((bf16[16,256,512]{2,1,0:T(8,128)(2,1)}), bf16[16,256,512]{2,1,0:T(8,128)(2,1)}, u32[]{:S(2)}, u32[]{:S(2)}) async-start(bf16[16,256,512]{2,1,0:T(8,128)(2,1)} %bitcast.59), calls=%async_computation | async-start | bytes 8388608 | tf_op jit(solution)/shard_map/all_to_all | solution.py:79
  8.8 0.1 convert_reduce_fusion
  8.9 0.0 copy-done
  8.9 0.7 fusion.51
  9.6 0.2 fusion.44
  9.8 18.2 %cosine_convert_fusion = (bf16[2048,512]{1,0:T(8,128)(2,1)S(1)}, bf16[2048,512]{1,0:T(8,128)(2,1)}) fusion(s32[512]{0:T(512)S(1)} %iota_add_fusion), kind=kLoop, calls=%fused_computation.19 | loop fusion | flops 17825792 | bytes 4196352 | tf_op jit(solution)/shard_map/convert.14
  28.0 57.6 %all-to-all-done = bf16[16,256,512]{2,1,0:T(8,128)(2,1)} async-done(((bf16[16,256,512]{2,1,0:T(8,128)(2,1)}), bf16[16,256,512]{2,1,0:T(8,128)(2,1)}, u32[]{:S(2)}, u32[]{:S(2)}) %all-to-all-start) | async-done | bytes 4194336 | tf_op jit(solution)/shard_map/all_to_all | solution.py:79
  85.5 6.4 %copy.11 = bf16[256,16,512]{0,2,1:T(8,128)(2,1)} copy(bf16[256,16,512]{2,0,1:T(8,128)(2,1)} %bitcast.2) | data formatting | bytes 8388608 | tf_op jit(solution)/shard_map/convert_element_type | solution.py:80
  91.9 5.2 %pad_convert_fusion = f32[256,8208]{0,1:T(8,128)} fusion(bf16[256,8192]{0,1:T(8,128)(2,1)} %bitcast.57), kind=kLoop, calls=%fused_computation.4 | loop fusion | flops 2101248 | bytes 12599296 | tf_op jit(solution)/shard_map/transpose | solution.py:26
  97.1 10.1 %reshape.192 = f32[256,2052,4]{0,2,1:T(4,128)} reshape(f32[256,8208]{0,1:T(8,128)} %pad_convert_fusion) | data formatting | bytes 16809984 | tf_op jit(solution)/shard_map/transpose | solution.py:26
  107.2 10.9 %copy.12 = f32[256,2052,4]{1,0,2:T(8,128)} copy(f32[256,2052,4]{0,2,1:T(4,128)} %reshape.192) | data formatting | bytes 16809984 | tf_op jit(solution)/shard_map/transpose | solution.py:26
  118.2 30.3 %fusion.3 = f32[256,1024]{1,0:T(8,128)S(1)} fusion(bf16[2048,512]{1,0:T(8,128)(2,1)} %get-tuple-element.16, bf16[2048,512]{1,0:T(8,128)(2,1)S(1)} %get-tuple-element.15, f32[4,256,2052]{2,1,0:T(8,128)} %bitcast.58, f32[256]{0:T(256)S(1)} %compare_convert_fusion, f32[]{:T(128)} %bitcast.19, f32[]{:T(128)} %bitcast.18, f32[]{:T(128)} %bitcast.17, ...), kind=kOutput, calls=%fused_computation.8 | convolution fusion | flops 1099431936 | bytes 38806528 | tf_op jit(solution)/shard_map/dot_general | solution.py:45
  148.4 0.7 fusion.49
  149.2 0.1 pad_maximum_fusion
  149.2 1.9 collective-permute-start
  151.2 1.3 collective-permute-start.1
  152.5 1.3 collective-permute-start.2
  153.8 1.3 collective-permute-start.3
  155.1 1.3 collective-permute-start.4
  156.4 1.1 subtract_convert_fusion
  157.5 0.1 maximum_dynamic-update-slice_fusion
  157.6 9.5 %collective-permute-done = bf16[256,1024]{1,0:T(8,128)(2,1)S(1)} collective-permute-done((bf16[256,1024]{1,0:T(8,128)(2,1)S(1)}, bf16[256,1024]{1,0:T(8,128)(2,1)S(1)}, u32[]{:S(2)}, u32[]{:S(2)}) %collective-permute-start) | collective-permute-done | bytes 524320 | tf_op jit(solution)/shard_map/ppermute | solution.py:19
  167.0 1.3 collective-permute-start.5
  168.4 3.1 %collective-permute-done.1 = bf16[256,1024]{1,0:T(8,128)(2,1)S(1)} collective-permute-done((bf16[256,1024]{1,0:T(8,128)(2,1)S(1)}, bf16[256,1024]{1,0:T(8,128)(2,1)S(1)}, u32[]{:S(2)}, u32[]{:S(2)}) %collective-permute-start.1) | collective-permute-done | bytes 524320 | tf_op jit(solution)/shard_map/ppermute | solution.py:19
  171.5 1.5 collective-permute-start.6
  173.0 25.6 %collective-permute-done.2 = bf16[256,1024]{1,0:T(8,128)(2,1)S(1)} collective-permute-done((bf16[256,1024]{1,0:T(8,128)(2,1)S(1)}, bf16[256,1024]{1,0:T(8,128)(2,1)S(1)}, u32[]{:S(2)}, u32[]{:S(2)}) %collective-permute-start.2) | collective-permute-done | bytes 524320 | tf_op jit(solution)/shard_map/ppermute | solution.py:19
  198.7 3.9 %collective-permute-done.3 = bf16[256,1024]{1,0:T(8,128)(2,1)S(1)} collective-permute-done((bf16[256,1024]{1,0:T(8,128)(2,1)S(1)}, bf16[256,1024]{1,0:T(8,128)(2,1)S(1)}, u32[]{:S(2)}, u32[]{:S(2)}) %collective-permute-start.3) | collective-permute-done | bytes 524320 | tf_op jit(solution)/shard_map/ppermute | solution.py:19
  202.6 2.3 collective-permute-done.4
  204.9 3.9 %collective-permute-done.5 = bf16[256,1024]{1,0:T(8,128)(2,1)S(1)} collective-permute-done((bf16[256,1024]{1,0:T(8,128)(2,1)S(1)}, bf16[256,1024]{1,0:T(8,128)(2,1)S(1)}, u32[]{:S(2)}, u32[]{:S(2)}) %collective-permute-start.5) | collective-permute-done | bytes 524320 | tf_op jit(solution)/shard_map/ppermute | solution.py:19
  208.8 62.8 %collective-permute-done.6 = bf16[256,1024]{1,0:T(8,128)(2,1)S(1)} collective-permute-done((bf16[256,1024]{1,0:T(8,128)(2,1)S(1)}, bf16[256,1024]{1,0:T(8,128)(2,1)S(1)}, u32[]{:S(2)}, u32[]{:S(2)}) %collective-permute-start.6) | collective-permute-done | bytes 524320 | tf_op jit(solution)/shard_map/ppermute | solution.py:19
  271.6 11.2 %multiply_convert_fusion = bf16[256,8,8,256]{3,0,2,1:T(8,128)(2,1)} fusion(f32[8]{0:T(128)S(1)} %compare_select_fusion.2, bf16[256,8,512]{2,0,1:T(8,128)(2,1)S(1)} %get-tuple-element.12, bf16[256,8,512]{2,0,1:T(8,128)(2,1)S(1)} %get-tuple-element.11, bf16[8,256,1024]{2,1,0:T(8,128)(2,1)S(1)} %bitcast_dynamic-update-slice_fusion), kind=kOutput, calls=%fused_computation | convolution fusion | flops 8606711808 | bytes 16777248 | tf_op jit(solution)/shard_map/dot_general | solution.py:94
  282.8 11.5 %copy.13 = bf16[256,8,8,256]{3,2,1,0:T(8,128)(2,1)} copy(bf16[256,8,8,256]{3,0,2,1:T(8,128)(2,1)} %multiply_convert_fusion) | data formatting | bytes 16777216 | tf_op jit(solution)/shard_map/convert_element_type | solution.py:98
  (11 shorter events, 0.3 us)
Async XLA Ops:
  0.0 8.9 %copy-start = (f32[16]{0:T(128)S(1)}, f32[16]{0:T(128)}, u32[]{:S(2)}) copy-start(f32[16]{0:T(128)} %param.5) | copy-start | bytes 196
  0.0 85.5 %all-to-all-start = ((bf16[16,256,512]{2,1,0:T(8,128)(2,1)}), bf16[16,256,512]{2,1,0:T(8,128)(2,1)}, u32[]{:S(2)}, u32[]{:S(2)}) async-start(bf16[16,256,512]{2,1,0:T(8,128)(2,1)} %bitcast.59), calls=%async_computation | async-start | bytes 8388608 | tf_op jit(solution)/shard_map/all_to_all | solution.py:79
  149.2 17.8 %collective-permute-start = (bf16[256,1024]{1,0:T(8,128)(2,1)S(1)}, bf16[256,1024]{1,0:T(8,128)(2,1)S(1)}, u32[]{:S(2)}, u32[]{:S(2)}) collective-permute-start(bf16[256,1024]{1,0:T(8,128)(2,1)S(1)} %pad_maximum_fusion), channel_id=1, source_target_pairs={{1,0},{2,1},{3,2},{4,3},{5,4},{6,5},{7,6},{8,7},{9,8},{10,9},{11,1... | collective-permute-start | bytes 1572872 | tf_op jit(solution)/shard_map/ppermute | solution.py:19
  151.2 20.3 %collective-permute-start.1 = (bf16[256,1024]{1,0:T(8,128)(2,1)S(1)}, bf16[256,1024]{1,0:T(8,128)(2,1)S(1)}, u32[]{:S(2)}, u32[]{:S(2)}) collective-permute-start(bf16[256,1024]{1,0:T(8,128)(2,1)S(1)} %pad_maximum_fusion), channel_id=1, source_target_pairs={{2,0},{3,1},{4,2},{5,3},{6,4},{7,5},{8,6},{9,7},{10,8},{11,9},{12,... | collective-permute-start | bytes 1572872 | tf_op jit(solution)/shard_map/ppermute | solution.py:19
  152.5 46.2 %collective-permute-start.2 = (bf16[256,1024]{1,0:T(8,128)(2,1)S(1)}, bf16[256,1024]{1,0:T(8,128)(2,1)S(1)}, u32[]{:S(2)}, u32[]{:S(2)}) collective-permute-start(bf16[256,1024]{1,0:T(8,128)(2,1)S(1)} %pad_maximum_fusion), channel_id=1, source_target_pairs={{3,0},{4,1},{5,2},{6,3},{7,4},{8,5},{9,6},{10,7},{11,8},{12,9},{13... | collective-permute-start | bytes 1572872 | tf_op jit(solution)/shard_map/ppermute | solution.py:19
  153.8 48.8 %collective-permute-start.3 = (bf16[256,1024]{1,0:T(8,128)(2,1)S(1)}, bf16[256,1024]{1,0:T(8,128)(2,1)S(1)}, u32[]{:S(2)}, u32[]{:S(2)}) collective-permute-start(bf16[256,1024]{1,0:T(8,128)(2,1)S(1)} %pad_maximum_fusion), channel_id=1, source_target_pairs={{4,0},{5,1},{6,2},{7,3},{8,4},{9,5},{10,6},{11,7},{12,8},{13,9},{1... | collective-permute-start | bytes 1572872 | tf_op jit(solution)/shard_map/ppermute | solution.py:19
  155.1 49.8 %collective-permute-start.4 = (bf16[256,1024]{1,0:T(8,128)(2,1)S(1)}, bf16[256,1024]{1,0:T(8,128)(2,1)S(1)}, u32[]{:S(2)}, u32[]{:S(2)}) collective-permute-start(bf16[256,1024]{1,0:T(8,128)(2,1)S(1)} %pad_maximum_fusion), channel_id=1, source_target_pairs={{5,0},{6,1},{7,2},{8,3},{9,4},{10,5},{11,6},{12,7},{13,8},{14,9},{... | collective-permute-start | bytes 1572872 | tf_op jit(solution)/shard_map/ppermute | solution.py:19
  167.0 41.8 %collective-permute-start.5 = (bf16[256,1024]{1,0:T(8,128)(2,1)S(1)}, bf16[256,1024]{1,0:T(8,128)(2,1)S(1)}, u32[]{:S(2)}, u32[]{:S(2)}) collective-permute-start(bf16[256,1024]{1,0:T(8,128)(2,1)S(1)} %pad_maximum_fusion), channel_id=1, source_target_pairs={{6,0},{7,1},{8,2},{9,3},{10,4},{11,5},{12,6},{13,7},{14,8},{15,9},... | collective-permute-start | bytes 1572872 | tf_op jit(solution)/shard_map/ppermute | solution.py:19
  171.5 100.1 %collective-permute-start.6 = (bf16[256,1024]{1,0:T(8,128)(2,1)S(1)}, bf16[256,1024]{1,0:T(8,128)(2,1)S(1)}, u32[]{:S(2)}, u32[]{:S(2)}) collective-permute-start(bf16[256,1024]{1,0:T(8,128)(2,1)S(1)} %pad_maximum_fusion), channel_id=1, source_target_pairs={{7,0},{8,1},{9,2},{10,3},{11,4},{12,5},{13,6},{14,7},{15,8},{23,16... | collective-permute-start | bytes 1572872 | tf_op jit(solution)/shard_map/ppermute | solution.py:19
where the time goes:
time: 295 us; the launch traced here: 294 us
  waiting for transfers between devices  169 us (57%)
  matrix products  42.2 us (14%)
  local copies, waits for them, and re-layouts  40 us (14%)
  other arithmetic  24.9 us (8%)
  starting transfers between devices  17.3 us (6%)
    ppermute x7, waiting for transfers between devices, from_behind(): lax.ppermute(value, axis, [(source, source + steps) for source in range(i...  111 us
    all_to_all x1, waiting for transfers between devices, shards(): lax.all_to_all(raw, 'row', split_axis=0, concat_axis=1, tiled=True)  57.6 us
    dot_general x1, matrix products, whiten(): jnp.dot(decimated, spectral_table(), preferred_element_type=jnp.float32)  30.3 us
    transpose x2, local copies, waits for them, and re-layouts, fir_decimate(): phased = jnp.transpose(padded.reshape(rows, width // DEC, DEC), (2, 0, 1))  21.1 us
    another operation x2, other arithmetic  19.3 us
    convert_element_type x1, local copies, waits for them, and re-layouts, shards(): return (shaped * scales[None, None, :, None]).astype(jnp.bfloat16)  11.5 us
    dot_general x1, matrix products, shards(): lax.dot_general(lagged, column_block, (((1,), (1,)), ((), ())), preferred...  11.2 us
    ppermute x7, starting transfers between devices, from_behind(): lax.ppermute(value, axis, [(source, source + steps) for source in range(i...  9.83 us
  transfers between devices with their start and end apart: 8, of which 8 were waited for; matrix products, arithmetic and copies ran while one was open for 7% of the time, Pallas kernels for 0%

commit v1 on v0

--- a/solution.py
+++ b/solution.py
@@ -76,7 +76,9 @@
 def shards(raw, fir_taps, band_width, dead_count):
     band_span = band_width[0]
     dead_here = dead_count[0]
-    channel_block = lax.all_to_all(raw, "row", split_axis=0, concat_axis=1, tiled=True)
+    channel_block = jnp.concatenate(
+        lax.all_to_all(jnp.stack(jnp.split(raw, lax.axis_size("row"), axis=0)), "row", 0, 0), axis=1
+    )
     padded = jnp.pad(channel_block.astype(jnp.float32), ((0, 0), (2 * DEC, 2 * DEC)))
     filtered = fir_decimate(padded, fir_taps, NT)
     tile_rows = filtered.shape[0]

time: 295 us -> 316 us (1.071)
  local copies, waits for them, and re-layouts: 40 us -> 59.9 us
    unnamed x8 -> x39, local copies, waits for them, and re-layouts: 0.22 us -> 22.6 us
    convert_element_type x1 -> x0, local copies, waits for them, and re-layouts: 6.38 us -> none  [shards(): channel_block.astype(jnp.float32)]
    split x0 -> x1, local copies, waits for them, and re-layouts: none -> 3.36 us  [shards(): jnp.split(raw, lax.axis_size('row'), axis=0)]
where the time goes in v1:
time: 316 us; the launch traced here: 315 us
  waiting for transfers between devices  169 us (53%)
  local copies, waits for them, and re-layouts  59.9 us (19%)
  matrix products  42.3 us (13%)
  other arithmetic  24.9 us (8%)
  starting transfers between devices  17.3 us (5%)
    ppermute x7, waiting for transfers between devices, from_behind(): lax.ppermute(value, axis, [(source, source + steps) for source in range(i...  111 us
    all_to_all x1, waiting for transfers between devices, shards(): lax.all_to_all(jnp.stack(jnp.split(raw, lax.axis_size('row'), axis=0)), '...  57.6 us
    dot_general x1, matrix products, whiten(): jnp.dot(decimated, spectral_table(), preferred_element_type=jnp.float32)  30.4 us
    unnamed x39, local copies, waits for them, and re-layouts  22.6 us
    transpose x2, local copies, waits for them, and re-layouts, fir_decimate(): phased = jnp.transpose(padded.reshape(rows, width // DEC, DEC), (2, 0, 1))  21 us
    another operation x2, other arithmetic  19.3 us
    convert_element_type x1, local copies, waits for them, and re-layouts, shards(): return (shaped * scales[None, None, :, None]).astype(jnp.bfloat16)  11.5 us
    dot_general x1, matrix products, shards(): lax.dot_general(lagged, column_block, (((1,), (1,)), ((), ())), preferred...  11.2 us
  transfers between devices with their start and end apart: 8, of which 8 were waited for; matrix products, arithmetic and copies ran while one was open for 7% of the time, Pallas kernels for 0%

profile of v1, /device:TPU:1, one launch (start us, length us, event | category | flops | bytes accessed | tf_op | source)
XLA Modules:
  0.0 314.6 jit_solution(7725385831266408182)
XLA Ops:
  0.0 3.4 %fusion.51 = (bf16[256,512]{1,0:T(8,128)(2,1)S(1)}, bf16[256,512]{1,0:T(8,128)(2,1)S(1)}, bf16[256,512]{1,0:T(8,128)(2,1)S(1)}, bf16[256,512]{1,0:T(8,128)(2,1)S...) fusion(bf16[4096,512]{1,0:T(8,128)(2,1)} %param.4), kind=kLoop, calls=%fused_computation.117 | loop fusion | bytes 8388608 | tf_op jit(solution)/shard_map/split | solution.py:80
  3.4 1.8 copy.59
  5.1 1.7 bitcast_dynamic-update-slice_fusion.22
  6.8 1.8 copy.60
  8.6 1.8 copy.61
  10.4 0.8 copy.62
  11.2 0.1 copy.63
  11.4 0.1 copy.64
  11.5 0.1 copy.65
  11.6 0.1 copy.66
  11.8 0.1 copy.67
  11.9 0.1 copy.68
  12.1 0.1 copy.69
  12.2 0.1 copy.70
  12.3 0.1 copy.71
  12.5 0.1 copy.72
  12.6 0.1 copy.73
  12.8 0.1 copy.74
  12.9 1.7 bitcast_dynamic-update-slice_fusion.21
  14.6 1.7 bitcast_dynamic-update-slice_fusion.20
  16.2 1.7 bitcast_dynamic-update-slice_fusion.19
  17.9 0.7 bitcast_dynamic-update-slice_fusion.18
  18.6 0.7 bitcast_dynamic-update-slice_fusion.17
  19.4 0.7 bitcast_dynamic-update-slice_fusion.16
  20.1 0.7 bitcast_dynamic-update-slice_fusion.15
  20.8 0.7 bitcast_dynamic-update-slice_fusion.14
  21.5 0.7 bitcast_dynamic-update-slice_fusion.13
  22.2 0.7 bitcast_dynamic-update-slice_fusion.12
  23.0 0.7 bitcast_dynamic-update-slice_fusion.11
  23.7 0.7 bitcast_dynamic-update-slice_fusion.10
  24.4 0.7 bitcast_dynamic-update-slice_fusion.9
  25.1 0.7 bitcast_dynamic-update-slice_fusion.8
  25.8 0.7 bitcast_dynamic-update-slice_fusion.7
  26.6 7.5 %all-to-all-start = ((bf16[16,256,512]{1,2,0:T(8,128)(2,1)}), bf16[16,256,512]{1,2,0:T(8,128)(2,1)}, u32[]{:S(2)}, u32[]{:S(2)}) async-start(bf16[16,256,512]{1,2,0:T(8,128)(2,1)} %bitcast_dynamic-update-slice_fusion.7), calls=%async_computation | async-start | bytes 8388608 | tf_op jit(solution)/shard_map/all_to_all | solution.py:80
  35.3 0.1 convert_reduce_fusion
  35.5 0.0 copy-done
  35.5 0.7 fusion.52
  36.2 0.2 fusion.44
  36.3 18.2 %cosine_convert_fusion = (bf16[2048,512]{1,0:T(8,128)(2,1)S(1)}, bf16[2048,512]{1,0:T(8,128)(2,1)}) fusion(s32[512]{0:T(512)S(1)} %iota_add_fusion), kind=kLoop, calls=%fused_computation.19 | loop fusion | flops 17825792 | bytes 4196352 | tf_op jit(solution)/shard_map/convert.14
  54.5 57.6 %all-to-all-done = bf16[16,256,512]{1,2,0:T(8,128)(2,1)} async-done(((bf16[16,256,512]{1,2,0:T(8,128)(2,1)}), bf16[16,256,512]{1,2,0:T(8,128)(2,1)}, u32[]{:S(2)}, u32[]{:S(2)}) %all-to-all-start) | async-done | bytes 4194336 | tf_op jit(solution)/shard_map/all_to_all | solution.py:80
  112.1 5.1 %pad_convert_fusion = f32[256,8208]{0,1:T(8,128)} fusion(bf16[256,8192]{0,1:T(8,128)(2,1)} %bitcast.18), kind=kLoop, calls=%fused_computation.4 | loop fusion | flops 2101248 | bytes 12599296 | tf_op jit(solution)/shard_map/transpose | solution.py:26
  117.3 10.1 %reshape.191 = f32[256,2052,4]{0,2,1:T(4,128)} reshape(f32[256,8208]{0,1:T(8,128)} %pad_convert_fusion) | data formatting | bytes 16809984 | tf_op jit(solution)/shard_map/transpose | solution.py:26
  127.4 10.8 %copy.56 = f32[256,2052,4]{1,0,2:T(8,128)} copy(f32[256,2052,4]{0,2,1:T(4,128)} %reshape.191) | data formatting | bytes 16809984 | tf_op jit(solution)/shard_map/transpose | solution.py:26
  138.2 30.4 %fusion.3 = f32[256,1024]{1,0:T(8,128)S(1)} fusion(bf16[2048,512]{1,0:T(8,128)(2,1)} %get-tuple-element.32, bf16[2048,512]{1,0:T(8,128)(2,1)S(1)} %get-tuple-element.31, f32[4,256,2052]{2,1,0:T(8,128)} %bitcast.89, f32[256]{0:T(256)S(1)} %compare_convert_fusion, f32[]{:T(128)} %bitcast.34, f32[]{:T(128)} %bitcast.33, f32[]{:T(128)} %bitcast.32, ...), kind=kOutput, calls=%fused_computation.8 | convolution fusion | flops 1099431936 | bytes 38806528 | tf_op jit(solution)/shard_map/dot_general | solution.py:45
  168.6 0.7 fusion.49
  169.4 0.1 pad_maximum_fusion
  169.4 1.9 collective-permute-start
  171.4 1.3 collective-permute-start.1
  172.7 1.3 collective-permute-start.2
  174.0 1.3 collective-permute-start.3
  175.3 1.5 collective-permute-start.4
  176.7 1.1 subtract_convert_fusion
  177.9 0.1 maximum_dynamic-update-slice_fusion
  177.9 9.3 %collective-permute-done = bf16[256,1024]{1,0:T(8,128)(2,1)S(1)} collective-permute-done((bf16[256,1024]{1,0:T(8,128)(2,1)S(1)}, bf16[256,1024]{1,0:T(8,128)(2,1)S(1)}, u32[]{:S(2)}, u32[]{:S(2)}) %collective-permute-start) | collective-permute-done | bytes 524320 | tf_op jit(solution)/shard_map/ppermute | solution.py:19
  187.3 1.3 collective-permute-start.5
  188.6 3.1 collective-permute-done.1
  191.7 1.3 collective-permute-start.6
  193.1 25.8 %collective-permute-done.2 = bf16[256,1024]{1,0:T(8,128)(2,1)S(1)} collective-permute-done((bf16[256,1024]{1,0:T(8,128)(2,1)S(1)}, bf16[256,1024]{1,0:T(8,128)(2,1)S(1)}, u32[]{:S(2)}, u32[]{:S(2)}) %collective-permute-start.2) | collective-permute-done | bytes 524320 | tf_op jit(solution)/shard_map/ppermute | solution.py:19
  218.9 3.9 %collective-permute-done.3 = bf16[256,1024]{1,0:T(8,128)(2,1)S(1)} collective-permute-done((bf16[256,1024]{1,0:T(8,128)(2,1)S(1)}, bf16[256,1024]{1,0:T(8,128)(2,1)S(1)}, u32[]{:S(2)}, u32[]{:S(2)}) %collective-permute-start.3) | collective-permute-done | bytes 524320 | tf_op jit(solution)/shard_map/ppermute | solution.py:19
  222.8 2.3 collective-permute-done.4
  225.2 3.9 %collective-permute-done.5 = bf16[256,1024]{1,0:T(8,128)(2,1)S(1)} collective-permute-done((bf16[256,1024]{1,0:T(8,128)(2,1)S(1)}, bf16[256,1024]{1,0:T(8,128)(2,1)S(1)}, u32[]{:S(2)}, u32[]{:S(2)}) %collective-permute-start.5) | collective-permute-done | bytes 524320 | tf_op jit(solution)/shard_map/ppermute | solution.py:19
  229.1 62.7 %collective-permute-done.6 = bf16[256,1024]{1,0:T(8,128)(2,1)S(1)} collective-permute-done((bf16[256,1024]{1,0:T(8,128)(2,1)S(1)}, bf16[256,1024]{1,0:T(8,128)(2,1)S(1)}, u32[]{:S(2)}, u32[]{:S(2)}) %collective-permute-start.6) | collective-permute-done | bytes 524320 | tf_op jit(solution)/shard_map/ppermute | solution.py:19
  291.8 11.2 %multiply_convert_fusion = bf16[256,8,8,256]{3,0,2,1:T(8,128)(2,1)} fusion(f32[8]{0:T(128)S(1)} %compare_select_fusion.2, bf16[256,8,512]{2,0,1:T(8,128)(2,1)S(1)} %get-tuple-element.28, bf16[256,8,512]{2,0,1:T(8,128)(2,1)S(1)} %get-tuple-element.27, bf16[8,256,1024]{2,1,0:T(8,128)(2,1)S(1)} %bitcast_dynamic-update-slice_fusion), kind=kOutput, calls=%fused_computation | convolution fusion | flops 8606711808 | bytes 16777248 | tf_op jit(solution)/shard_map/dot_general | solution.py:96
  303.0 11.5 %copy.57 = bf16[256,8,8,256]{3,2,1,0:T(8,128)(2,1)} copy(bf16[256,8,8,256]{3,0,2,1:T(8,128)(2,1)} %multiply_convert_fusion) | data formatting | bytes 16777216 | tf_op jit(solution)/shard_map/convert_element_type | solution.py:100
  (12 shorter events, 0.3 us)
Async XLA Ops:
  26.6 8.9 %copy-start = (f32[16]{0:T(128)S(1)}, f32[16]{0:T(128)}, u32[]{:S(2)}) copy-start(f32[16]{0:T(128)} %param.5) | copy-start | bytes 196
  26.6 85.5 %all-to-all-start = ((bf16[16,256,512]{1,2,0:T(8,128)(2,1)}), bf16[16,256,512]{1,2,0:T(8,128)(2,1)}, u32[]{:S(2)}, u32[]{:S(2)}) async-start(bf16[16,256,512]{1,2,0:T(8,128)(2,1)} %bitcast_dynamic-update-slice_fusion.7), calls=%async_computation | async-start | bytes 8388608 | tf_op jit(solution)/shard_map/all_to_all | solution.py:80
  169.4 17.8 %collective-permute-start = (bf16[256,1024]{1,0:T(8,128)(2,1)S(1)}, bf16[256,1024]{1,0:T(8,128)(2,1)S(1)}, u32[]{:S(2)}, u32[]{:S(2)}) collective-permute-start(bf16[256,1024]{1,0:T(8,128)(2,1)S(1)} %pad_maximum_fusion), channel_id=1, source_target_pairs={{1,0},{2,1},{3,2},{4,3},{5,4},{6,5},{7,6},{8,7},{9,8},{10,9},{11,1... | collective-permute-start | bytes 1572872 | tf_op jit(solution)/shard_map/ppermute | solution.py:19
  171.4 20.4 %collective-permute-start.1 = (bf16[256,1024]{1,0:T(8,128)(2,1)S(1)}, bf16[256,1024]{1,0:T(8,128)(2,1)S(1)}, u32[]{:S(2)}, u32[]{:S(2)}) collective-permute-start(bf16[256,1024]{1,0:T(8,128)(2,1)S(1)} %pad_maximum_fusion), channel_id=1, source_target_pairs={{2,0},{3,1},{4,2},{5,3},{6,4},{7,5},{8,6},{9,7},{10,8},{11,9},{12,... | collective-permute-start | bytes 1572872 | tf_op jit(solution)/shard_map/ppermute | solution.py:19
  172.7 46.2 %collective-permute-start.2 = (bf16[256,1024]{1,0:T(8,128)(2,1)S(1)}, bf16[256,1024]{1,0:T(8,128)(2,1)S(1)}, u32[]{:S(2)}, u32[]{:S(2)}) collective-permute-start(bf16[256,1024]{1,0:T(8,128)(2,1)S(1)} %pad_maximum_fusion), channel_id=1, source_target_pairs={{3,0},{4,1},{5,2},{6,3},{7,4},{8,5},{9,6},{10,7},{11,8},{12,9},{13... | collective-permute-start | bytes 1572872 | tf_op jit(solution)/shard_map/ppermute | solution.py:19
  174.0 48.8 %collective-permute-start.3 = (bf16[256,1024]{1,0:T(8,128)(2,1)S(1)}, bf16[256,1024]{1,0:T(8,128)(2,1)S(1)}, u32[]{:S(2)}, u32[]{:S(2)}) collective-permute-start(bf16[256,1024]{1,0:T(8,128)(2,1)S(1)} %pad_maximum_fusion), channel_id=1, source_target_pairs={{4,0},{5,1},{6,2},{7,3},{8,4},{9,5},{10,6},{11,7},{12,8},{13,9},{1... | collective-permute-start | bytes 1572872 | tf_op jit(solution)/shard_map/ppermute | solution.py:19
  175.3 49.9 %collective-permute-start.4 = (bf16[256,1024]{1,0:T(8,128)(2,1)S(1)}, bf16[256,1024]{1,0:T(8,128)(2,1)S(1)}, u32[]{:S(2)}, u32[]{:S(2)}) collective-permute-start(bf16[256,1024]{1,0:T(8,128)(2,1)S(1)} %pad_maximum_fusion), channel_id=1, source_target_pairs={{5,0},{6,1},{7,2},{8,3},{9,4},{10,5},{11,6},{12,7},{13,8},{14,9},{... | collective-permute-start | bytes 1572872 | tf_op jit(solution)/shard_map/ppermute | solution.py:19
  187.3 41.8 %collective-permute-start.5 = (bf16[256,1024]{1,0:T(8,128)(2,1)S(1)}, bf16[256,1024]{1,0:T(8,128)(2,1)S(1)}, u32[]{:S(2)}, u32[]{:S(2)}) collective-permute-start(bf16[256,1024]{1,0:T(8,128)(2,1)S(1)} %pad_maximum_fusion), channel_id=1, source_target_pairs={{6,0},{7,1},{8,2},{9,3},{10,4},{11,5},{12,6},{13,7},{14,8},{15,9},... | collective-permute-start | bytes 1572872 | tf_op jit(solution)/shard_map/ppermute | solution.py:19
  191.7 100.1 %collective-permute-start.6 = (bf16[256,1024]{1,0:T(8,128)(2,1)S(1)}, bf16[256,1024]{1,0:T(8,128)(2,1)S(1)}, u32[]{:S(2)}, u32[]{:S(2)}) collective-permute-start(bf16[256,1024]{1,0:T(8,128)(2,1)S(1)} %pad_maximum_fusion), channel_id=1, source_target_pairs={{7,0},{8,1},{9,2},{10,3},{11,4},{12,5},{13,6},{14,7},{15,8},{23,16... | collective-permute-start | bytes 1572872 | tf_op jit(solution)/shard_map/ppermute | solution.py:19
